TPU v7x, 32 devices: a whole 2x2x4 slice. The times are simulated.
32 devices in a mesh: grp: 1, dev: 32 (over z, y, x, core).
Axes of the slice: x: 2, y: 2, z: 4, core: 2. Of those that a mesh axis runs over, the one named last changes fastest.
Arguments:
- hidden_in: bfloat16 [640, 32, 768], P(('grp', 'dev')), may hold values from -6 to 6
- grad_out: bfloat16 [640, 32, 768], P(('grp', 'dev')), may hold values from -6 to 6
- norm_gain: float32 [768], replicated, may hold values from 0.25 to 1.75
- w_qkv: bfloat16 [768, 2304], replicated, may hold values from -0.21875 to 0.21875
- w_out: bfloat16 [768, 768], replicated, may hold values from -0.21875 to 0.21875
- sharpness: float32 [12], replicated, may hold values from 4 to 20
- cohort_ids: int32 [640], P('grp'), may hold values from 0 to 3
- observed: int32 [640, 32], P('grp', 'dev'), may hold values 0 or 1
Outputs:
- grad_in: bfloat16 [640, 32, 768], P(('grp', 'dev'))
- grad_qkv: float32 [768, 2304], P(('grp', 'dev'))
- grad_wout: float32 [768, 768], P(('grp', 'dev'))
All inputs are finite; a program needn't handle non-finite values. No bound on the sum of `observed` on one device may be relied on, other than what follows from the above.
Results may differ from a plain program's by a relative error of at most 0.015.
Values may be sent and summed in bfloat16 or wider, within the bound.
A program may use at most 128 MiB of HBM per device.

v0:
```python
import jax
import jax.numpy as jnp
from jax import lax
from jax.sharding import PartitionSpec as P

epsilon = 1e-06


def row_sum(left, right):
    return lax.dot_general(
        left, right, (((0,), (0,)), ((), ())), preferred_element_type=jnp.float32
    )


def forward_part(rows_in, norm_gain, w_qkv, heads):
    campaigns, patches, width = rows_in.shape
    head_size = width // heads
    values = rows_in.astype(jnp.float32)
    inv_rms = lax.rsqrt(jnp.mean(values * values, axis=-1, keepdims=True) + epsilon)
    unit_rows = values * inv_rms
    normed = (unit_rows * norm_gain).astype(jnp.bfloat16).reshape(-1, width)
    projected = jnp.dot(normed, w_qkv, preferred_element_type=jnp.float32)
    shape4 = (campaigns, patches, heads, head_size)
    query_raw = projected[:, :width].reshape(shape4)
    key_raw = projected[:, width : 2 * width].reshape(shape4)
    value_half = projected[:, 2 * width :].reshape(shape4).astype(jnp.bfloat16)
    query_inv = lax.rsqrt(jnp.mean(query_raw * query_raw, axis=-1, keepdims=True) + epsilon)
    key_inv = lax.rsqrt(jnp.mean(key_raw * key_raw, axis=-1, keepdims=True) + epsilon)
    query_unit = query_raw * query_inv
    key_unit = key_raw * key_inv
    return (
        inv_rms,
        unit_rows,
        normed,
        query_unit,
        query_inv,
        key_unit,
        key_inv,
        query_unit.astype(jnp.bfloat16),
        key_unit.astype(jnp.bfloat16),
        value_half,
    )


def body(hidden_in, grad_out, norm_gain, w_qkv, w_out, sharpness, cohort_ids, observed):
    heads = sharpness.shape[0]
    rows_in, grad_rows = (
        lax.all_to_all(hidden_in, "dev", split_axis=1, concat_axis=0, tiled=True),
        lax.all_to_all(grad_out, "dev", split_axis=1, concat_axis=0, tiled=True),
    )
    forward = forward_part(rows_in, norm_gain, w_qkv, heads)
    (
        inv_rms,
        unit_rows,
        normed,
        query_unit,
        query_inv,
        key_unit,
        key_inv,
        query_half,
        key_half,
        value_half,
    ) = forward
    campaigns, patches, width = rows_in.shape
    head_size = width // heads
    shape4 = (campaigns, patches, heads, head_size)
    dy_rows = grad_rows.reshape(-1, width)
    grad_attn = lax.dot_general(
        dy_rows, w_out, (((1,), (1,)), ((), ())), preferred_element_type=jnp.float32
    )
    grad_attn = grad_attn.astype(jnp.bfloat16).reshape(shape4)
    same = cohort_ids[:, None] == cohort_ids[None, :]
    diagonal = jnp.eye(campaigns, dtype=bool)
    keys_seen = (observed.T == 1)[:, None, :]
    allowed = jnp.where(same[None] & (keys_seen | diagonal[None]), 1.0, 0.0).astype(jnp.float32)

    def head_step(index, carry):
        attended, grad_qunit, grad_kunit, grad_value = carry
        query_head = lax.dynamic_index_in_dim(query_half, index, 2, keepdims=False)
        key_head = lax.dynamic_index_in_dim(key_half, index, 2, keepdims=False)
        value_head = lax.dynamic_index_in_dim(value_half, index, 2, keepdims=False)
        grad_head = lax.dynamic_index_in_dim(grad_attn, index, 2, keepdims=False)
        scale = lax.dynamic_index_in_dim(sharpness, index, 0, keepdims=False) / head_size
        scores = (
            jnp.einsum("ipe,jpe->pij", query_head, key_head, preferred_element_type=jnp.float32)
            * scale
        )
        raw_weights = jnp.exp(scores) * allowed
        probs = raw_weights / jnp.sum(raw_weights, axis=-1, keepdims=True)
        probs_half = probs.astype(jnp.bfloat16)
        out_head = jnp.einsum(
            "pij,jpe->ipe", probs_half, value_head, preferred_element_type=jnp.float32
        )
        grad_probs = jnp.einsum(
            "ipe,jpe->pij", grad_head, value_head, preferred_element_type=jnp.float32
        )
        value_grad = jnp.einsum(
            "pij,ipe->jpe", probs_half, grad_head, preferred_element_type=jnp.float32
        )
        row_dot = jnp.sum(grad_probs * probs, axis=-1, keepdims=True)
        grad_scores = (probs * (grad_probs - row_dot) * scale).astype(jnp.bfloat16)
        qunit_head = jnp.einsum(
            "pij,jpe->ipe", grad_scores, key_head, preferred_element_type=jnp.float32
        )
        kunit_head = jnp.einsum(
            "pij,ipe->jpe", grad_scores, query_head, preferred_element_type=jnp.float32
        )
        return (
            lax.dynamic_update_index_in_dim(attended, out_head, index, 2),
            lax.dynamic_update_index_in_dim(grad_qunit, qunit_head, index, 2),
            lax.dynamic_update_index_in_dim(grad_kunit, kunit_head, index, 2),
            lax.dynamic_update_index_in_dim(grad_value, value_grad, index, 2),
        )

    empty = jnp.zeros(shape4, jnp.float32)
    attended, grad_qunit, grad_kunit, grad_value = lax.fori_loop(
        0, heads, head_step, (empty, empty, empty, empty)
    )
    grad_query = query_inv * (
        grad_qunit - query_unit * jnp.mean(grad_qunit * query_unit, axis=-1, keepdims=True)
    )
    grad_key = key_inv * (
        grad_kunit - key_unit * jnp.mean(grad_kunit * key_unit, axis=-1, keepdims=True)
    )
    grad_proj = jnp.concatenate(
        [grad_query.reshape(-1, width), grad_key.reshape(-1, width), grad_value.reshape(-1, width)],
        axis=1,
    ).astype(jnp.bfloat16)
    attended_half = attended.astype(jnp.bfloat16).reshape(-1, width)
    out_term = row_sum(attended_half, dy_rows)
    grad_wout = lax.psum_scatter(
        out_term.astype(jnp.bfloat16), "dev", scatter_dimension=0, tiled=True
    ).astype(jnp.float32)
    grad_normed = lax.dot_general(
        grad_proj, w_qkv, (((1,), (1,)), ((), ())), preferred_element_type=jnp.float32
    )
    shaped = grad_normed.reshape(campaigns, patches, width) * norm_gain
    result = grad_rows.astype(jnp.float32) + inv_rms * (
        shaped - unit_rows * jnp.mean(shaped * unit_rows, axis=-1, keepdims=True)
    )
    grad_in = lax.all_to_all(
        result.astype(jnp.bfloat16), "dev", split_axis=0, concat_axis=1, tiled=True
    )
    grad_qkv = lax.psum_scatter(
        row_sum(normed, grad_proj).astype(jnp.bfloat16), "dev", scatter_dimension=0, tiled=True
    ).astype(jnp.float32)
    return (grad_in, grad_qkv, grad_wout)


def solution(mesh):
    in_specs = (
        P(("grp", "dev"), None, None),
        P(("grp", "dev"), None, None),
        P(),
        P(),
        P(),
        P(),
        P("grp"),
        P("grp", "dev"),
    )
    out_specs = (P(("grp", "dev"), None, None), P(("grp", "dev"), None), P(("grp", "dev"), None))
    return jax.shard_map(body, mesh=mesh, in_specs=in_specs, out_specs=out_specs, check_vma=False)
```

profile of v0, /device:TPU:0, one launch (start us, length us, event | category | flops | bytes accessed | tf_op | source)
XLA Modules:
  0.0 459.8 jit_solution(5012240428037647978)
XLA Ops:
  7.2 2.9 copy.28
  10.1 7.4 %all-to-all-start.1 = ((bf16[20,32,768]{2,0,1:T(8,128)(2,1)}), bf16[20,32,768]{2,0,1:T(8,128)(2,1)}, u32[]{:S(2)}, u32[]{:S(2)}) async-start(bf16[20,32,768]{2,0,1:T(8,128)(2,1)} %copy.28), calls=%async_computation.1 | async-start | bytes 2359296 | tf_op jit(solution)/shard_map/all_to_all | solution.py:48
  17.6 2.8 copy.27
  21.0 25.6 %all-to-all-done.1 = bf16[20,32,768]{2,0,1:T(8,128)(2,1)} async-done(((bf16[20,32,768]{2,0,1:T(8,128)(2,1)}), bf16[20,32,768]{2,0,1:T(8,128)(2,1)}, u32[]{:S(2)}, u32[]{:S(2)}) %all-to-all-start.1) | async-done | bytes 983072 | tf_op jit(solution)/shard_map/all_to_all | solution.py:48
  46.5 3.7 all-to-all-start
  52.6 2.9 convert_bitcast_fusion
  56.1 2.7 reshape.437
  60.3 4.1 fusion.38
  65.4 2.3 fusion.40
  67.7 2.9 copy.33
  70.5 2.9 copy.31
  73.4 2.2 copy.32
  79.3 2.1 all_to_all.36
  81.4 3.5 convolution_convert_fusion.2
  85.0 2.2 copy.34
  87.2 3.9 multiply_convert_fusion.4
  91.1 145.6 %while.20 = (s32[]{:T(128)}, bf16[640,1,12,64]{0,3,2,1:T(8,128)(2,1)}, f32[640,1,12,64]{0,3,2,1:T(8,128)}, f32[640,1,12,64]{0,3,2,1:T(8,128)}, bf16[640,1,12,64]...) while((s32[]{:T(128)}, ...), condition=%wide.region_6.7_spmd.clone, body=%wide.region_3.6_spmd.clone.sunk | while | flops 322763520 | bytes 15271073 | solution.py:116
  95.8 1.9 fusion.73
  108.0 1.9 fusion.73
  111.7 1.9 fusion.74
  120.1 1.9 fusion.73
  123.9 1.9 fusion.74
  132.2 1.9 fusion.73
  144.3 1.9 fusion.73
  156.5 1.9 fusion.73
  168.6 1.9 fusion.73
  172.4 1.9 fusion.74
  180.7 2.0 fusion.73
  192.9 1.9 fusion.73
  205.0 1.9 fusion.73
  217.1 1.9 fusion.73
  220.9 1.9 fusion.74
  229.3 1.9 fusion.73
  233.0 1.9 fusion.74
  236.8 3.2 multiply_reduce_fusion.3
  241.3 3.3 convolution_convert_fusion.1
  246.4 2.7 multiply_convert_fusion.2
  252.0 6.2 %convolution_convert_fusion = bf16[768,2304]{1,0:T(8,128)(2,1)} fusion(bf16[640,768]{0,1:T(8,128)(2,1)} %bitcast.11, bf16[640,768]{0,1:T(8,128)(2,1)S(1)} %bitcast.138, bf16[640,768]{0,1:T(8,128)(2,1)S(1)} %bitcast.136, f32[640,768]{1,0:T(8,128)S(1)} %copy-done.4, f32[768]{0:T(1024)S(1)} %copy-done.16, f32[640]{0:T(1024)S(1)} %copy-done.15), kind=kOutput, calls=%fused_computation.41 | convolution fusion | flops 2277015552 | bytes 8459776 | tf_op jit(solution)/shard_map/dot_general | solution.py:10
  258.3 5.5 %multiply_reduce_fusion.1 = (f32[640]{0:T(1024)S(1)}, f32[640,768]{1,0:T(8,128)S(1)}) fusion(f32[640,768]{1,0:T(8,128)} %reshape.437, f32[768]{0:T(1024)S(1)} %copy-done.16, f32[640]{0:T(1024)S(1)} %copy-done.15, bf16[768,2304]{1,0:T(8,128)(2,1)S(1)} %copy-done, bf16[640,768]{0,1:T(8,128)(2,1)} %bitcast.11, bf16[640,768]{0,1:T(8,128)(2,1)} %bitcast.139, ...), kind=kOutput, calls=%fused_computation.48 | convolution fusion | flops 2275737088 | bytes 10428416 | tf_op jit(solution)/shard_map/dot_general | solution.py:134
  265.8 3.3 reduce.21
  269.0 3.3 reshape.446
  272.3 6.0 %all-to-all-start.2 = ((bf16[32,2,7680]{2,1,0:T(2,128)(2,1)}), bf16[32,2,7680]{2,1,0:T(2,128)(2,1)}, u32[]{:S(2)}, u32[]{:S(2)}) async-start(bf16[32,2,7680]{2,1,0:T(2,128)(2,1)} %reshape.446), calls=%async_computation.2 | async-start | bytes 1966080 | tf_op jit(solution)/shard_map/all_to_all | solution.py:141
  278.3 65.1 %reduce-scatter.5.cloned.1.call-done = bf16[24,768]{1,0:T(8,128)(2,1)} async-done(((bf16[768,768]{1,0:T(8,128)(2,1)}), bf16[24,768]{1,0:T(8,128)(2,1)}) %reduce-scatter.5.cloned.1.call-update) | async-done | bytes 36880 | tf_op jit(solution)/shard_map/reduce_scatter | solution.py:131
  344.8 5.6 %reshape.447 = bf16[640,1,768]{2,1,0:T(2,128)(2,1)} reshape(bf16[32,2,7680]{2,1,0:T(2,128)(2,1)} %all-to-all-done.2) | data formatting | bytes 1966080
  350.5 7.9 %reduce.19 = bf16[640,768]{1,0:T(8,128)(2,1)} reduce(bf16[640,1,768]{2,1,0:T(2,128)(2,1)} %reshape.447, bf16[]{:T(256)} %constant.84), dimensions={1}, to_apply=%all_to_all.38.reduce_sub_computation | reduce | bytes 1966082 | tf_op jit(solution)/shard_map/all_to_all | solution.py:141
  358.4 2.2 all_to_all.39
  360.6 2.4 copy.36
  363.0 88.4 %reduce-scatter.3.cloned.1.call-done = bf16[24,2304]{1,0:T(8,128)(2,1)} async-done(((bf16[768,2304]{1,0:T(8,128)(2,1)}), bf16[24,2304]{1,0:T(8,128)(2,1)}) %reduce-scatter.3.cloned.1.call-update) | async-done | bytes 110608 | tf_op jit(solution)/shard_map/reduce_scatter | solution.py:144
  (151 shorter events, 125.6 us)
Async XLA Ops:
  7.2 53.1 %copy-start = (bf16[768,2304]{1,0:T(8,128)(2,1)S(1)}, bf16[768,2304]{1,0:T(8,128)(2,1)}, u32[]{:S(2)}) copy-start(bf16[768,2304]{1,0:T(8,128)(2,1)} %param.13) | copy-start | bytes 10616836
  10.1 10.3 %copy-start.17 = (s32[640,1]{0,1:T(1,128)S(1)}, s32[640,1]{0,1:T(1,128)}, u32[]{:S(2)}) copy-start(s32[640,1]{0,1:T(1,128)} %param.17) | copy-start | bytes 7684
  10.1 36.5 %all-to-all-start.1 = ((bf16[20,32,768]{2,0,1:T(8,128)(2,1)}), bf16[20,32,768]{2,0,1:T(8,128)(2,1)}, u32[]{:S(2)}, u32[]{:S(2)}) async-start(bf16[20,32,768]{2,0,1:T(8,128)(2,1)} %copy.28), calls=%async_computation.1 | async-start | bytes 2359296 | tf_op jit(solution)/shard_map/all_to_all | solution.py:48
  46.5 32.7 %all-to-all-start = ((bf16[20,32,768]{2,0,1:T(8,128)(2,1)}), bf16[20,32,768]{2,0,1:T(8,128)(2,1)}, u32[]{:S(2)}, u32[]{:S(2)}) async-start(bf16[20,32,768]{2,0,1:T(8,128)(2,1)} %copy.27), calls=%async_computation | async-start | bytes 2359296 | tf_op jit(solution)/shard_map/all_to_all | solution.py:49
  50.3 293.1 %reduce-scatter.5.cloned.1.call-start = ((), (), s32[]{:S(2)}) async-start(), calls=%async_computation.6 | async-start | bytes 1216512 | tf_op jit(solution)/shard_map/reduce_scatter | solution.py:131
  52.6 2.9 copy-start.14
  75.6 2.1 copy-start.3
  87.2 3.9 copy-start.18
  87.2 3.9 copy-start.19
  87.2 3.9 copy-start.20
  236.7 3.2 copy-start.1
  236.8 3.3 copy-start.6
  236.8 3.3 copy-start.12
  240.1 1.2 copy-start.8
  244.6 206.7 %reduce-scatter.3.cloned.1.call-start = ((), (), s32[]{:S(2)}) async-start(), calls=%async_computation.5 | async-start | bytes 3649536 | tf_op jit(solution)/shard_map/reduce_scatter | solution.py:144
  246.4 2.7 copy-start.2
  246.4 3.3 copy-start.7
  246.4 3.3 copy-start.13
  249.8 1.0 copy-start.10
  249.8 2.3 copy-start.4
  249.8 2.3 copy-start.15
  249.8 2.3 copy-start.16
  250.2 0.9 copy-start.11
  258.2 5.5 %copy-start.5 = (f32[640,768]{1,0:T(8,128)S(1)}, f32[640,768]{1,0:T(8,128)}, u32[]{:S(2)}) copy-start(f32[640,768]{1,0:T(8,128)} %reshape.437) | copy-start | bytes 5898244
  258.2 5.5 %copy-start.9 = (bf16[640,768]{1,0:T(8,128)(2,1)S(1)}, bf16[640,768]{1,0:T(8,128)(2,1)}, u32[]{:S(2)}) copy-start(bf16[640,768]{1,0:T(8,128)(2,1)} %all_to_all.36) | copy-start | bytes 2949124
  272.3 72.6 %all-to-all-start.2 = ((bf16[32,2,7680]{2,1,0:T(2,128)(2,1)}), bf16[32,2,7680]{2,1,0:T(2,128)(2,1)}, u32[]{:S(2)}, u32[]{:S(2)}) async-start(bf16[32,2,7680]{2,1,0:T(2,128)(2,1)} %reshape.446), calls=%async_computation.2 | async-start | bytes 1966080 | tf_op jit(solution)/shard_map/all_to_all | solution.py:141
Sparse Core Ops, SparseCore 0:
  244.8 98.6 reduce-scatter.4
  348.8 102.4 reduce-scatter.2
where the time goes:
time: 464 us; the launch traced here: 460 us
  waiting for transfers between devices  179 us (39%)
  matrix products  149 us (32%)
  local copies, waits for them, and re-layouts  50.9 us (11%)
  other arithmetic  41.2 us (9%)
  starting transfers between devices  17.5 us (4%)
  between operations  14.2 us (3%)
  loops' own time  7.86 us (2%)
    reduce_scatter x1, waiting for transfers between devices, body(): lax.psum_scatter(row_sum(normed, grad_proj).astype(jnp.bfloat16), 'dev',...  88.4 us
    reduce_scatter x1, waiting for transfers between devices, body(): lax.psum_scatter(out_term.astype(jnp.bfloat16), 'dev', scatter_dimension=...  65.1 us
    all_to_all x1, waiting for transfers between devices, body(): lax.all_to_all(hidden_in, 'dev', split_axis=1, concat_axis=0, tiled=True)  25.6 us
    dot_general x12, matrix products, head_step(): jnp.einsum('pij,ipe->jpe', grad_scores, query_head, preferred_element_typ...  23.3 us
    dot_general x12, matrix products, head_step(): jnp.einsum('pij,ipe->jpe', probs_half, grad_head, preferred_element_type=...  22.9 us
    dot_general x12, matrix products, head_step(): jnp.einsum('pij,jpe->ipe', grad_scores, key_head, preferred_element_type=...  21.9 us
    dot_general x12, matrix products, head_step(): jnp.einsum('pij,jpe->ipe', probs_half, value_head, preferred_element_type...  21.6 us
    unnamed x48, local copies, waits for them, and re-layouts  20.8 us
  transfers between devices with their start and end apart: 5, of which 4 were waited for; matrix products, arithmetic and copies ran while one was open for 16% of the time, Pallas kernels for 0%

commit v1 on v0

--- a/solution.py
+++ b/solution.py
@@ -45,7 +45,12 @@
 def body(hidden_in, grad_out, norm_gain, w_qkv, w_out, sharpness, cohort_ids, observed):
     heads = sharpness.shape[0]
     rows_in, grad_rows = (
-        lax.all_to_all(hidden_in, "dev", split_axis=1, concat_axis=0, tiled=True),
+        jnp.concatenate(
+            lax.all_to_all(
+                jnp.stack(jnp.split(hidden_in, lax.axis_size("dev"), axis=1)), "dev", 0, 0
+            ),
+            axis=0,
+        ),
         lax.all_to_all(grad_out, "dev", split_axis=1, concat_axis=0, tiled=True),
     )
     forward = forward_part(rows_in, norm_gain, w_qkv, heads)

time: 464 us -> 491 us (1.058)
  local copies, waits for them, and re-layouts: 50.9 us -> 78.6 us
  waiting for transfers between devices: 179 us -> 184 us
    unnamed x48 -> x75, local copies, waits for them, and re-layouts: 20.8 us -> 36.5 us
    dynamic_slice x12, local copies, waits for them, and re-layouts: 7.6 us -> 15.4 us  [head_step(): lax.dynamic_index_in_dim(sharpness, index, 0, keepdims=False) / head_size]
    all_to_all x1, waiting for transfers between devices: 0.09 us -> 5.06 us  [body(): lax.all_to_all(grad_out, 'dev', split_axis=1, concat_axis=0, tiled=True)]
  transfers between devices with their start and end apart: 5 -> 5, of which waited for: 4 -> 4; matrix products, arithmetic and copies ran while one was open for 16% -> 14% of each run, Pallas kernels for 0% -> 0%
where the time goes in v1:
time: 491 us; the launch traced here: 487 us
  waiting for transfers between devices  184 us (37%)
  matrix products  149 us (30%)
  local copies, waits for them, and re-layouts  78.6 us (16%)
  other arithmetic  37.7 us (8%)
  starting transfers between devices  15.6 us (3%)
  between operations  14.3 us (3%)
  loops' own time  7.84 us (2%)
    reduce_scatter x1, waiting for transfers between devices, body(): lax.psum_scatter(row_sum(normed, grad_proj).astype(jnp.bfloat16), 'dev',...  88.4 us
    reduce_scatter x1, waiting for transfers between devices, body(): lax.psum_scatter(out_term.astype(jnp.bfloat16), 'dev', scatter_dimension=...  65.1 us
    unnamed x75, local copies, waits for them, and re-layouts  36.5 us
    all_to_all x1, waiting for transfers between devices, body(): lax.all_to_all(jnp.stack(jnp.split(hidden_in, lax.axis_size('dev'), axis=...  25.6 us
    dot_general x12, matrix products, head_step(): jnp.einsum('pij,ipe->jpe', grad_scores, query_head, preferred_element_typ...  23.3 us
    dot_general x12, matrix products, head_step(): jnp.einsum('pij,ipe->jpe', probs_half, grad_head, preferred_element_type=...  22.9 us
    dot_general x12, matrix products, head_step(): jnp.einsum('pij,jpe->ipe', grad_scores, key_head, preferred_element_type=...  21.8 us
    dot_general x12, matrix products, head_step(): jnp.einsum('pij,jpe->ipe', probs_half, value_head, preferred_element_type...  21.6 us
  transfers between devices with their start and end apart: 5, of which 4 were waited for; matrix products, arithmetic and copies ran while one was open for 14% of the time, Pallas kernels for 0%

profile of v1, /device:TPU:0, one launch (start us, length us, event | category | flops | bytes accessed | tf_op | source)
XLA Modules:
  0.0 487.0 jit_solution(8816637736598797060)
XLA Ops:
  7.2 3.6 fusion.41
  31.6 7.4 %all-to-all-start.1 = ((bf16[32,20,1,768]{3,1,2,0:T(8,128)(2,1)}), bf16[32,20,1,768]{3,1,2,0:T(8,128)(2,1)}, u32[]{:S(2)}, u32[]{:S(2)}) async-start(bf16[32,20,1,768]{3,1,2,0:T(8,128)(2,1)} %constant_dynamic-update-slice_fusion), calls=%async_computation.1 | async-start | bytes 2359296 | tf_op jit(solution)/shard_map/all_to_all | solution.py:49
  39.1 2.8 copy.88
  42.4 25.6 %all-to-all-done.1 = bf16[32,20,1,768]{3,1,2,0:T(8,128)(2,1)} async-done(((bf16[32,20,1,768]{3,1,2,0:T(8,128)(2,1)}), bf16[32,20,1,768]{3,1,2,0:T(8,128)(2,1)}, u32[]{:S(2)}, u32[]{:S(2)}) %all-to-all-start.1) | async-done | bytes 983072 | tf_op jit(solution)/shard_map/all_to_all | solution.py:49
  68.0 3.7 all-to-all-start
  74.3 2.5 reshape.434
  76.8 4.1 fusion.37
  81.9 2.3 fusion.39
  84.2 2.9 copy.123
  87.0 2.9 copy.121
  89.9 2.2 copy.122
  95.7 5.1 %all-to-all-done = bf16[20,32,768]{2,0,1:T(8,128)(2,1)} async-done(((bf16[20,32,768]{2,0,1:T(8,128)(2,1)}), bf16[20,32,768]{2,0,1:T(8,128)(2,1)}, u32[]{:S(2)}, u32[]{:S(2)}) %all-to-all-start) | async-done | bytes 983072 | tf_op jit(solution)/shard_map/all_to_all | solution.py:54
  100.8 2.1 all_to_all.32
  102.9 3.5 convolution_convert_fusion.2
  106.4 2.2 copy.124
  108.7 3.9 multiply_convert_fusion.4
  112.6 153.4 %while.20 = (s32[]{:T(128)}, bf16[640,1,12,64]{0,3,2,1:T(8,128)(2,1)}, f32[640,1,12,64]{0,3,2,1:T(8,128)}, f32[640,1,12,64]{0,3,2,1:T(8,128)}, bf16[640,1,12,64]...) while((s32[]{:T(128)}, ...), condition=%wide.region_6.7_spmd.clone, body=%wide.region_3.6_spmd.clone.sunk | while | flops 322763520 | bytes 15271073 | solution.py:121
  117.9 1.9 fusion.74
  121.7 1.9 fusion.75
  130.7 1.9 fusion.74
  143.5 1.9 fusion.74
  147.2 1.9 fusion.75
  156.2 1.9 fusion.74
  169.0 1.9 fusion.74
  181.8 2.0 fusion.74
  194.6 1.9 fusion.74
  198.3 1.9 fusion.75
  207.4 1.9 fusion.74
  220.2 1.9 fusion.74
  232.9 1.9 fusion.74
  245.7 1.9 fusion.74
  249.5 1.9 fusion.75
  258.5 1.9 fusion.74
  262.3 1.9 fusion.75
  266.0 3.2 multiply_reduce_fusion.4
  270.5 3.3 convolution_convert_fusion.1
  275.7 2.7 multiply_convert_fusion.2
  281.3 6.2 %convolution_convert_fusion = bf16[768,2304]{1,0:T(8,128)(2,1)} fusion(bf16[640,768]{0,1:T(8,128)(2,1)} %bitcast.40, bf16[640,768]{0,1:T(8,128)(2,1)S(1)} %bitcast.260, bf16[640,768]{0,1:T(8,128)(2,1)S(1)} %bitcast.258, f32[640,768]{1,0:T(8,128)S(1)} %copy-done.4, f32[768]{0:T(1024)S(1)} %copy-done.16, f32[640]{0:T(1024)S(1)} %copy-done.15), kind=kOutput, calls=%fused_computation.41 | convolution fusion | flops 2277015552 | bytes 8459776 | tf_op jit(solution)/shard_map/dot_general | solution.py:10
  287.5 5.5 %multiply_reduce_fusion.2 = (f32[640]{0:T(1024)S(1)}, f32[640,768]{1,0:T(8,128)S(1)}) fusion(f32[640,768]{1,0:T(8,128)} %reshape.434, f32[768]{0:T(1024)S(1)} %copy-done.16, f32[640]{0:T(1024)S(1)} %copy-done.15, bf16[768,2304]{1,0:T(8,128)(2,1)S(1)} %copy-done, bf16[640,768]{0,1:T(8,128)(2,1)} %bitcast.40, bf16[640,768]{0,1:T(8,128)(2,1)} %bitcast.261, ...), kind=kOutput, calls=%fused_computation.46 | convolution fusion | flops 2275737088 | bytes 10428416 | tf_op jit(solution)/shard_map/dot_general | solution.py:139
  295.0 3.2 reduce.19
  298.3 3.3 reshape.442
  301.6 4.0 all-to-all-start.2
  305.5 65.1 %reduce-scatter.5.cloned.1.call-done = bf16[24,768]{1,0:T(8,128)(2,1)} async-done(((bf16[768,768]{1,0:T(8,128)(2,1)}), bf16[24,768]{1,0:T(8,128)(2,1)}) %reduce-scatter.5.cloned.1.call-update) | async-done | bytes 36880 | tf_op jit(solution)/shard_map/reduce_scatter | solution.py:136
  372.0 5.6 %reshape.443 = bf16[640,1,768]{2,1,0:T(2,128)(2,1)} reshape(bf16[32,2,7680]{2,1,0:T(2,128)(2,1)} %all-to-all-done.2) | data formatting | bytes 1966080
  377.7 7.9 %reduce.17 = bf16[640,768]{1,0:T(8,128)(2,1)} reduce(bf16[640,1,768]{2,1,0:T(2,128)(2,1)} %reshape.443, bf16[]{:T(256)} %constant.84), dimensions={1}, to_apply=%all_to_all.34.reduce_sub_computation | reduce | bytes 1966082 | tf_op jit(solution)/shard_map/all_to_all | solution.py:146
  385.6 2.2 all_to_all.35
  387.7 2.4 copy.126
  390.2 88.4 %reduce-scatter.3.cloned.1.call-done = bf16[24,2304]{1,0:T(8,128)(2,1)} async-done(((bf16[768,2304]{1,0:T(8,128)(2,1)}), bf16[24,2304]{1,0:T(8,128)(2,1)}) %reduce-scatter.3.cloned.1.call-update) | async-done | bytes 110608 | tf_op jit(solution)/shard_map/reduce_scatter | solution.py:149
  (179 shorter events, 152.3 us)
Async XLA Ops:
  7.2 69.6 %copy-start = (bf16[768,2304]{1,0:T(8,128)(2,1)S(1)}, bf16[768,2304]{1,0:T(8,128)(2,1)}, u32[]{:S(2)}) copy-start(bf16[768,2304]{1,0:T(8,128)(2,1)} %param.13) | copy-start | bytes 10616836
  7.2 3.6 copy-start.10
  31.6 36.5 %all-to-all-start.1 = ((bf16[32,20,1,768]{3,1,2,0:T(8,128)(2,1)}), bf16[32,20,1,768]{3,1,2,0:T(8,128)(2,1)}, u32[]{:S(2)}, u32[]{:S(2)}) async-start(bf16[32,20,1,768]{3,1,2,0:T(8,128)(2,1)} %constant_dynamic-update-slice_fusion), calls=%async_computation.1 | async-start | bytes 2359296 | tf_op jit(solution)/shard_map/all_to_all | solution.py:49
  39.0 2.8 copy-start.17
  68.0 32.7 %all-to-all-start = ((bf16[20,32,768]{2,0,1:T(8,128)(2,1)}), bf16[20,32,768]{2,0,1:T(8,128)(2,1)}, u32[]{:S(2)}, u32[]{:S(2)}) async-start(bf16[20,32,768]{2,0,1:T(8,128)(2,1)} %copy.88), calls=%async_computation | async-start | bytes 2359296 | tf_op jit(solution)/shard_map/all_to_all | solution.py:54
  71.8 298.8 %reduce-scatter.5.cloned.1.call-start = ((), (), s32[]{:S(2)}) async-start(), calls=%async_computation.6 | async-start | bytes 1216512 | tf_op jit(solution)/shard_map/reduce_scatter | solution.py:136
  74.3 2.5 copy-start.15
  74.3 2.5 copy-start.16
  92.1 2.1 copy-start.3
  108.7 3.9 copy-start.18
  108.7 3.9 copy-start.19
  266.0 3.2 copy-start.1
  266.0 3.3 copy-start.6
  266.0 3.3 copy-start.13
  269.3 1.2 copy-start.8
  273.9 204.7 %reduce-scatter.3.cloned.1.call-start = ((), (), s32[]{:S(2)}) async-start(), calls=%async_computation.5 | async-start | bytes 3649536 | tf_op jit(solution)/shard_map/reduce_scatter | solution.py:149
  275.7 2.7 copy-start.2
  275.7 3.4 copy-start.7
  275.7 3.4 copy-start.14
  279.1 1.0 copy-start.11
  279.1 2.3 copy-start.4
  279.5 0.9 copy-start.12
  287.5 5.5 %copy-start.5 = (f32[640,768]{1,0:T(8,128)S(1)}, f32[640,768]{1,0:T(8,128)}, u32[]{:S(2)}) copy-start(f32[640,768]{1,0:T(8,128)} %reshape.434) | copy-start | bytes 5898244
  287.5 5.5 %copy-start.9 = (bf16[640,768]{1,0:T(8,128)(2,1)S(1)}, bf16[640,768]{1,0:T(8,128)(2,1)}, u32[]{:S(2)}) copy-start(bf16[640,768]{1,0:T(8,128)(2,1)} %all_to_all.32) | copy-start | bytes 2949124
  301.6 70.5 %all-to-all-start.2 = ((bf16[32,2,7680]{2,1,0:T(2,128)(2,1)}), bf16[32,2,7680]{2,1,0:T(2,128)(2,1)}, u32[]{:S(2)}, u32[]{:S(2)}) async-start(bf16[32,2,7680]{2,1,0:T(2,128)(2,1)} %reshape.442), calls=%async_computation.2 | async-start | bytes 1966080 | tf_op jit(solution)/shard_map/all_to_all | solution.py:146
Sparse Core Ops, SparseCore 0:
  274.0 96.5 reduce-scatter.4
  376.0 102.4 reduce-scatter.2
